TPU v7x, 32 devices: a whole 2x2x4 slice. The times are simulated.
32 devices in a mesh: wa: 4 (over z), ha: 8 (over y, x, core).
Axes of the slice: x: 2, y: 2, z: 4, core: 2. Of those that a mesh axis runs over, the one named last changes fastest.
Arguments:
- tokens: bfloat16 [1024, 16384], P('ha', 'wa'), may hold values from -6 to 6
- gain_attn: bfloat16 [16384], P('wa'), may hold values from 0.25 to 1.75
- w_query: bfloat16 [16384, 16384], P('wa', 'ha'), may hold values from -0.046875 to 0.046875, as said below
- w_key: bfloat16 [16384, 1024], P('wa'), may hold values from -1.171875 to 1.171875, as said below
- w_value: bfloat16 [16384, 1024], P('wa'), may hold values from -0.046875 to 0.046875
- w_out: bfloat16 [16384, 16384], P('ha', 'wa'), may hold values from -0.1875 to 0.1875
- gain_ffn: bfloat16 [16384], P('wa'), may hold values from 0.25 to 1.75
- segment_ids: int32 [1024], replicated, may hold values from 0 to 31, never falling along the last dimension, each value on 1 to 256 neighbouring positions
Outputs:
- residual_out: bfloat16 [1024, 16384], P('ha', 'wa')
- ffn_input: bfloat16 [1024, 16384], P('ha', 'wa')
Inputs may be any that keep to these rules, and one draw needn't show every extreme that they name: `w_query`: entries scaled by 16384 ** -0.5. `w_key`: entries scaled by 16384 ** -0.5. `segment_ids`: segment ids never fall along the tokens; each prompt has 1 to 256 tokens and one has exactly 256.
All inputs are finite; a program needn't handle non-finite values.
Results may differ from a plain program's by a relative error of at most 0.00675.
The roundings to bfloat16 on the way count: a program that leaves them out, or rounds other values in their place, can miss the bound.
Values may be sent and summed in bfloat16 or wider, within the bound.
A program may use at most 192 MiB of HBM per device.

v0:
```python
import jax
import jax.numpy as jnp
from jax import lax
from jax.sharding import PartitionSpec as P

KVH = 8
HD = 128
WINDOW = 256
EPS = 1e-05


def rope_tables(position):
    half = HD // 2
    inverse = 500000.0 ** (-(jnp.arange(half, dtype=jnp.float32) * 2.0 / HD))
    angle = position[:, None] * inverse[None, :]
    return (jnp.cos(angle), jnp.sin(angle))


def rotate(values, cosine, sine):
    half = values.shape[-1] // 2
    first = values[..., :half]
    second = values[..., half:]
    cosine = cosine[:, None, :]
    sine = sine[:, None, :]
    return jnp.concatenate(
        [first * cosine - second * sine, second * cosine + first * sine], axis=-1
    )


def attend(queries, key_head, value_head, segment_ids, first):
    q_rows = queries.shape[0]
    size = min(WINDOW, q_rows)
    keys_pad = jnp.pad(key_head, ((WINDOW, 0), (0, 0)))
    values_pad = jnp.pad(value_head, ((WINDOW, 0), (0, 0)))
    segment_pad = jnp.pad(segment_ids, (WINDOW, 0), constant_values=-1)
    outs = []
    for at in range(0, q_rows, size):
        start = first + at
        query = queries[at : at + size]
        key = lax.dynamic_slice_in_dim(keys_pad, start, size + WINDOW, 0)
        value = lax.dynamic_slice_in_dim(values_pad, start, size + WINDOW, 0)
        k_segment = lax.dynamic_slice_in_dim(segment_pad, start, size + WINDOW, 0)
        q_segment = lax.dynamic_slice_in_dim(segment_ids, start, size, 0)
        k_at = jnp.arange(size + WINDOW, dtype=jnp.int32) - WINDOW
        q_at = jnp.arange(size, dtype=jnp.int32)
        allowed = (q_segment[:, None] == k_segment[None, :]) & (k_at[None, :] <= q_at[:, None])
        allowed = allowed & (k_at + start >= 0)[None, :]
        scores = jnp.einsum("thd,sd->hts", query, key, preferred_element_type=jnp.float32) * HD ** (
            -0.5
        )
        scores = jnp.where(allowed[None], scores, -1e30)
        peak = jnp.max(scores, axis=-1, keepdims=True)
        expo = jnp.where(allowed[None], jnp.exp(scores - peak), 0.0)
        weights = (expo / jnp.sum(expo, axis=-1, keepdims=True)).astype(jnp.bfloat16)
        out = jnp.einsum("hts,sd->thd", weights, value, preferred_element_type=jnp.float32)
        outs.append(out.astype(jnp.bfloat16))
    return jnp.concatenate(outs, axis=0)


def on_device(tokens, gain_attn, w_query, w_key, w_value, w_out, gain_ffn, segment_ids):
    rows_dev, width_dev = tokens.shape
    n_wa = lax.axis_size("wa")
    n_ha = lax.axis_size("ha")
    total = rows_dev * n_ha
    width = width_dev * n_wa
    head_cols = w_query.shape[1]
    heads_dev = head_cols // HD
    token_f = tokens.astype(jnp.float32)
    gain_one = gain_attn.astype(jnp.float32)
    kv_head = lax.axis_index("ha") // (n_ha // KVH)
    kv_weights = jnp.concatenate(
        [
            lax.dynamic_slice_in_dim(w_key, kv_head * HD, HD, 1),
            lax.dynamic_slice_in_dim(w_value, kv_head * HD, HD, 1),
        ],
        axis=1,
    )
    gathered = lax.all_gather(tokens, "ha", axis=0, tiled=True)
    gathered_f = gathered.astype(jnp.float32)
    row_sq = jnp.sum(gathered_f * gathered_f, axis=1)
    scaled = (gathered_f * gain_one).astype(jnp.bfloat16)
    kv_part = jnp.dot(scaled, kv_weights, preferred_element_type=jnp.float32)
    kv_sum = lax.psum(
        jnp.concatenate([kv_part, jnp.broadcast_to(row_sq[:, None], (total, HD))], axis=1), "wa"
    )
    row_scale = lax.rsqrt(kv_sum[:, 2 * HD] / width + EPS)
    index_all = jnp.arange(total, dtype=jnp.int32)
    fresh = jnp.concatenate([jnp.ones((1,), dtype=bool), segment_ids[1:] != segment_ids[:-1]])
    start_all = lax.cummax(jnp.where(fresh, index_all, jnp.zeros_like(index_all)), axis=0)
    cosine, sine = rope_tables((index_all - start_all).astype(jnp.float32))
    key_plain = (kv_sum[:, :HD] * row_scale[:, None]).astype(jnp.bfloat16)
    key_plain = lax.optimization_barrier(key_plain)
    value_head = (kv_sum[:, HD : 2 * HD] * row_scale[:, None]).astype(jnp.bfloat16)
    key_head = rotate(key_plain.astype(jnp.float32).reshape(total, 1, HD), cosine, sine)
    key_head = key_head.reshape(total, HD).astype(jnp.bfloat16)
    q_rows = total // n_wa
    first = lax.axis_index("wa") * q_rows
    block = scaled
    query_f = lax.psum_scatter(
        jnp.dot(block, w_query, preferred_element_type=jnp.float32),
        "wa",
        scatter_dimension=0,
        tiled=True,
    )
    q_scale = lax.dynamic_slice_in_dim(row_scale, first, q_rows, 0)
    q_cos = lax.dynamic_slice_in_dim(cosine, first, q_rows, 0)
    q_sin = lax.dynamic_slice_in_dim(sine, first, q_rows, 0)
    queries = rotate(
        (query_f * q_scale[:, None]).reshape(q_rows, heads_dev, HD), q_cos, q_sin
    ).astype(jnp.bfloat16)
    head_out = attend(queries, key_head, value_head, segment_ids, first)
    head_out = head_out.reshape(q_rows, head_cols)
    head_all = lax.all_gather(head_out, "wa", axis=0, tiled=True)
    block = head_all
    attended = lax.psum_scatter(
        jnp.dot(block, w_out, preferred_element_type=jnp.float32).astype(jnp.bfloat16),
        "ha",
        scatter_dimension=0,
        tiled=True,
    )
    residual_out = (token_f + attended.astype(jnp.float32)).astype(jnp.bfloat16)
    residual_f = residual_out.astype(jnp.float32)
    square_two = lax.psum(jnp.sum(residual_f * residual_f, axis=1), "wa")
    scale_two = lax.rsqrt(square_two / width + EPS)
    ffn_input = (residual_f * scale_two[:, None] * gain_ffn.astype(jnp.float32)).astype(
        jnp.bfloat16
    )
    return (residual_out, ffn_input)


def solution(mesh):
    in_specs = (
        P("ha", "wa"),
        P("wa"),
        P("wa", "ha"),
        P("wa", None),
        P("wa", None),
        P("ha", "wa"),
        P("wa"),
        P(),
    )
    out_specs = (P("ha", "wa"), P("ha", "wa"))
    return jax.shard_map(
        on_device, mesh=mesh, in_specs=in_specs, out_specs=out_specs, check_vma=False
    )
```

profile of v0, /device:TPU:0, one launch (start us, length us, event | category | flops | bytes accessed | tf_op | source)
XLA Modules:
  0.0 499.1 jit_solution(17607958058642940988)
XLA Ops:
  7.2 0.7 all-gather.3.cloned.1.call-update
  7.9 0.7 convert_element_type.63
  8.7 1.7 constant_dynamic-slice_fusion.1
  10.3 56.5 %all-gather.3.cloned.1.call-done = bf16[1024,4096]{1,0:T(8,128)(2,1)} async-done(((bf16[128,4096]{1,0:T(8,128)(2,1)}), bf16[1024,4096]{1,0:T(8,128)(2,1)}) %all-gather.3.cloned.1.call-update) | async-done | bytes 8388624 | tf_op jit(solution)/shard_map/all_gather | solution.py:78
  66.9 5.2 %fusion.2 = f32[1024]{0:T(1024)S(1)} fusion(bf16[1024,4096]{1,0:T(8,128)(2,1)} %all-gather.3.cloned.1.call-done), kind=kLoop, calls=%fused_computation.4 | loop fusion | flops 12581888 | bytes 8392704 | tf_op jit(solution)/shard_map/reduce_sum | solution.py:80
  72.1 0.5 copy-done
  72.6 2.4 fusion.5
  75.1 1.3 pad_maximum_fusion
  76.5 24.1 %fusion.3 = f32[1024,2048]{1,0:T(8,128)} fusion(bf16[4096,2048]{1,0:T(8,128)(2,1)} %param.10, bf16[1024,4096]{1,0:T(8,128)(2,1)} %all-gather.3.cloned.1.call-done, f32[4096]{0:T(1024)S(1)} %convert_element_type.63), kind=kOutput, calls=%fused_computation.9 | convolution fusion | flops 17192452096 | bytes 33570816 | tf_op jit(solution)/shard_map/dot_general | solution.py:100
  100.8 0.4 copy-done.3
  101.4 0.3 reduce-window.9
  102.4 0.5 dynamic-slice_cosine_fusion
  102.8 0.3 fusion.26
  103.1 42.5 %all-reduce.5.cloned.1.call-done = f32[1024,384]{0,1:T(8,128)} async-done(((f32[1024,384]{0,1:T(8,128)}), f32[1024,384]{0,1:T(8,128)}) %all-reduce.5.cloned.1.call-update) | async-done | bytes 1572880 | tf_op jit(solution)/shard_map/psum | solution.py:83
  145.6 0.8 fusion.40
  146.3 1.3 fusion.24
  147.7 1.2 fusion.32
  148.9 142.8 %reduce-scatter.3.cloned.1.call-done = f32[256,2048]{1,0:T(8,128)} async-done(((f32[1024,2048]{1,0:T(8,128)}), f32[256,2048]{1,0:T(8,128)}) %reduce-scatter.3.cloned.1.call-update) | async-done | bytes 2097168 | tf_op jit(solution)/shard_map/reduce_scatter | solution.py:99
  291.7 1.8 multiply_bitcast_fusion
  293.5 0.4 copy.23
  293.9 0.7 fusion.50
  294.6 1.4 subtract_convert_fusion
  296.0 1.3 fusion.19
  297.3 4.3 fusion.51
  301.6 1.7 fusion.18
  303.7 81.0 %all-gather.5.cloned.1.call-done = bf16[1024,2048]{0,1:T(8,128)(2,1)} async-done(((bf16[256,2048]{0,1:T(8,128)(2,1)}), bf16[1024,2048]{0,1:T(8,128)(2,1)}) %all-gather.5.cloned.1.call-update) | async-done | bytes 4194320 | tf_op jit(solution)/shard_map/all_gather | solution.py:113
  384.7 23.2 %convolution_convert_fusion = bf16[1024,4096]{1,0:T(8,128)(2,1)} fusion(bf16[1024,2048]{0,1:T(8,128)(2,1)} %all-gather.5.cloned.1.call-done, bf16[2048,4096]{1,0:T(8,128)(2,1)} %param.13), kind=kOutput, calls=%fused_computation.8 | convolution fusion | flops 17184063488 | bytes 29360128 | tf_op jit(solution)/shard_map/dot_general | solution.py:116
  408.0 0.7 copy-done.4
  408.7 69.2 %reduce-scatter.5.cloned.1.call-done = bf16[128,4096]{1,0:T(8,128)(2,1)} async-done(((bf16[1024,4096]{1,0:T(8,128)(2,1)}), bf16[128,4096]{1,0:T(8,128)(2,1)}) %reduce-scatter.5.cloned.1.call-update) | async-done | bytes 1048592 | tf_op jit(solution)/shard_map/reduce_scatter | solution.py:115
  477.8 1.7 fusion.12
  479.5 11.7 %psum.15 = f32[128]{0:T(128)S(1)} all-reduce(f32[128]{0:T(128)S(1)} %get-tuple-element.2), channel_id=1, replica_groups=mesh['wa'=4,'ha'=8] {'wa'}, use_global_device_ids=true, to_apply=%region_9.10 | all-reduce | flops 128 | bytes 1024 | tf_op jit(solution)/shard_map/psum | solution.py:123
  491.2 1.3 fusion.14
  (33 shorter events, 1.6 us)
Async XLA Ops:
  7.2 59.7 %all-gather.3.cloned.1.call-start = ((), (), s32[]{:S(2)}) async-start(), calls=%async_computation.2 | async-start | bytes 9437184 | tf_op jit(solution)/shard_map/all_gather | solution.py:78
  7.9 137.7 %all-reduce.5.cloned.1.call-start = ((), (), s32[]{:S(2)}) async-start(), calls=%async_computation.3 | async-start | bytes 3145728 | tf_op jit(solution)/shard_map/psum | solution.py:83
  66.9 5.8 %copy-start = (bf16[1024,4096]{1,0:T(8,128)(2,1)S(1)}, bf16[1024,4096]{1,0:T(8,128)(2,1)}, u32[]{:S(2)}) copy-start(bf16[1024,4096]{1,0:T(8,128)(2,1)} %all-gather.3.cloned.1.call-done) | copy-start | bytes 25165828
  76.4 215.3 %reduce-scatter.3.cloned.1.call-start = ((), (), s32[]{:S(2)}) async-start(), calls=%async_computation.4 | async-start | bytes 10485760 | tf_op jit(solution)/shard_map/reduce_scatter | solution.py:99
  100.6 0.7 copy-start.3
  100.6 284.1 %all-gather.5.cloned.1.call-start = ((), (), s32[]{:S(2)}) async-start(), calls=%async_computation.5 | async-start | bytes 5242880 | tf_op jit(solution)/shard_map/all_gather | solution.py:113
  303.4 174.4 %reduce-scatter.5.cloned.1.call-start = ((), (), s32[]{:S(2)}) async-start(), calls=%async_computation.6 | async-start | bytes 9437184 | tf_op jit(solution)/shard_map/reduce_scatter | solution.py:115
  408.0 0.7 copy-start.4
  408.0 69.9 %copy-start.2 = (bf16[128,4096]{1,0:T(8,128)(2,1)S(1)}, bf16[128,4096]{1,0:T(8,128)(2,1)}, u32[]{:S(2)}) copy-start(bf16[128,4096]{1,0:T(8,128)(2,1)} %param.8) | copy-start | bytes 3145732
  479.5 13.0 %copy-start.1 = (bf16[128,4096]{1,0:T(8,128)(2,1)}, bf16[128,4096]{1,0:T(8,128)(2,1)S(1)}, u32[]{:S(2)}) copy-start(bf16[128,4096]{1,0:T(8,128)(2,1)S(1)} %get-tuple-element.3) | copy-start | bytes 3145732
Sparse Core Ops, SparseCore 0:
  9.9 56.9 all-gather.2
  76.6 68.9 all-reduce.4
  147.9 143.7 reduce-scatter.2
  303.5 81.1 all-gather.4
  408.1 69.6 reduce-scatter.4
where the time goes:
time: 499 us
  waiting for transfers between devices  393 us (79%)
  matrix products  52.8 us (11%)
  other arithmetic  22.1 us (4%)
  between operations  13.9 us (3%)
  blocking collectives  11.7 us (2%)
  local copies, waits for them, and re-layouts  5.19 us (1%)
    reduce_scatter x1, waiting for transfers between devices, on_device(): lax.psum_scatter(jnp.dot(block, w_query, preferred_element_type=jnp.float...  143 us
    all_gather x1, waiting for transfers between devices, on_device(): head_all = lax.all_gather(head_out, 'wa', axis=0, tiled=True)  81 us
    reduce_scatter x1, waiting for transfers between devices, on_device(): lax.psum_scatter(jnp.dot(block, w_out, preferred_element_type=jnp.float32...  69.2 us
    all_gather x1, waiting for transfers between devices, on_device(): gathered = lax.all_gather(tokens, 'ha', axis=0, tiled=True)  56.5 us
    psum x1, waiting for transfers between devices, on_device(): lax.psum(jnp.concatenate([kv_part, jnp.broadcast_to(row_sq[:, None], (tot...  42.5 us
    dot_general x1, matrix products, on_device(): jnp.dot(block, w_query, preferred_element_type=jnp.float32)  24.1 us
    dot_general x1, matrix products, on_device(): jnp.dot(block, w_out, preferred_element_type=jnp.float32)  23.2 us
    psum x1, blocking collectives, on_device(): square_two = lax.psum(jnp.sum(residual_f * residual_f, axis=1), 'wa')  11.7 us
  transfers between devices with their start and end apart: 5, of which 5 were waited for; matrix products, arithmetic and copies ran while one was open for 6% of the time, Pallas kernels for 0%

commit v1 on v0

--- a/solution.py
+++ b/solution.py
@@ -80,9 +80,9 @@
     row_sq = jnp.sum(gathered_f * gathered_f, axis=1)
     scaled = (gathered_f * gain_one).astype(jnp.bfloat16)
     kv_part = jnp.dot(scaled, kv_weights, preferred_element_type=jnp.float32)
-    kv_sum = lax.psum(
-        jnp.concatenate([kv_part, jnp.broadcast_to(row_sq[:, None], (total, HD))], axis=1), "wa"
-    )
+    part = jnp.concatenate([kv_part, jnp.broadcast_to(row_sq[:, None], (total, HD))], axis=1)
+    terms = lax.all_gather(part, "wa")
+    kv_sum = jnp.sum(terms, axis=0)
     row_scale = lax.rsqrt(kv_sum[:, 2 * HD] / width + EPS)
     index_all = jnp.arange(total, dtype=jnp.int32)
     fresh = jnp.concatenate([jnp.ones((1,), dtype=bool), segment_ids[1:] != segment_ids[:-1]])

time: 499 us -> 545 us (1.092)
  waiting for transfers between devices: 393 us -> 425 us
  local copies, waits for them, and re-layouts: 5.19 us -> 13.9 us
    all_gather x0 -> x1, waiting for transfers between devices: none -> 88.8 us  [on_device(): terms = lax.all_gather(part, 'wa')]
    psum x1 -> x0, waiting for transfers between devices: 42.5 us -> none  [on_device(): lax.psum(jnp.concatenate([kv_part, jnp.broadcast_to(row_sq[:, None], (tot...]
    reduce_scatter x1, waiting for transfers between devices: 143 us -> 129 us  [on_device(): lax.psum_scatter(jnp.dot(block, w_query, preferred_element_type=jnp.float...]
    all_gather x0 -> x1, local copies, waits for them, and re-layouts: none -> 8.54 us  [on_device(): terms = lax.all_gather(part, 'wa')]
    reduce_sum x0 -> x1, other arithmetic: none -> 6.61 us  [on_device(): kv_sum = jnp.sum(terms, axis=0)]
  transfers between devices with their start and end apart: 5 -> 5, of which waited for: 5 -> 5; matrix products, arithmetic and copies ran while one was open for 6% -> 8% of each run, Pallas kernels for 0% -> 0%
where the time goes in v1:
time: 545 us
  waiting for transfers between devices  425 us (78%)
  matrix products  52.8 us (10%)
  other arithmetic  26.9 us (5%)
  local copies, waits for them, and re-layouts  13.9 us (3%)
  between operations  13.9 us (3%)
  blocking collectives  11.7 us (2%)
    reduce_scatter x1, waiting for transfers between devices, on_device(): lax.psum_scatter(jnp.dot(block, w_query, preferred_element_type=jnp.float...  129 us
    all_gather x1, waiting for transfers between devices, on_device(): terms = lax.all_gather(part, 'wa')  88.8 us
    all_gather x1, waiting for transfers between devices, on_device(): head_all = lax.all_gather(head_out, 'wa', axis=0, tiled=True)  81.3 us
    reduce_scatter x1, waiting for transfers between devices, on_device(): lax.psum_scatter(jnp.dot(block, w_out, preferred_element_type=jnp.float32...  69.2 us
    all_gather x1, waiting for transfers between devices, on_device(): gathered = lax.all_gather(tokens, 'ha', axis=0, tiled=True)  56.5 us
    dot_general x1, matrix products, on_device(): jnp.dot(block, w_query, preferred_element_type=jnp.float32)  24.1 us
    dot_general x1, matrix products, on_device(): jnp.dot(block, w_out, preferred_element_type=jnp.float32)  23.2 us
    psum x1, blocking collectives, on_device(): square_two = lax.psum(jnp.sum(residual_f * residual_f, axis=1), 'wa')  11.7 us
  transfers between devices with their start and end apart: 5, of which 5 were waited for; matrix products, arithmetic and copies ran while one was open for 8% of the time, Pallas kernels for 0%

profile of v1, /device:TPU:0, one launch (start us, length us, event | category | flops | bytes accessed | tf_op | source)
XLA Modules:
  0.0 544.6 jit_solution(12266972876900854344)
XLA Ops:
  7.2 0.7 all-gather.5.cloned.1.call-update
  7.9 0.7 convert_element_type.63
  8.6 1.7 constant_dynamic-slice_fusion.1
  10.3 56.5 %all-gather.5.cloned.1.call-done = bf16[1024,4096]{1,0:T(8,128)(2,1)} async-done(((bf16[128,4096]{1,0:T(8,128)(2,1)}), bf16[1024,4096]{1,0:T(8,128)(2,1)}) %all-gather.5.cloned.1.call-update) | async-done | bytes 8388624 | tf_op jit(solution)/shard_map/all_gather | solution.py:78
  66.9 5.2 fusion.2
  72.1 0.5 copy-done
  72.6 2.4 fusion.5
  75.1 1.3 pad_maximum_fusion
  76.5 24.1 %fusion.3 = f32[1024,2048]{1,0:T(8,128)} fusion(bf16[4096,2048]{1,0:T(8,128)(2,1)} %param.10, bf16[1024,4096]{1,0:T(8,128)(2,1)} %all-gather.5.cloned.1.call-done, f32[4096]{0:T(1024)S(1)} %convert_element_type.63), kind=kOutput, calls=%fused_computation.9 | convolution fusion | flops 17192452096 | bytes 33570816 | tf_op jit(solution)/shard_map/dot_general | solution.py:100
  100.6 0.6 copy-done.3
  101.4 0.3 reduce-window.9
  102.4 0.5 dynamic-slice_cosine_fusion
  102.8 0.3 fusion.26
  103.1 88.8 %all-gather.9.cloned.1.call-done = f32[4096,384]{0,1:T(8,128)} async-done(((f32[1024,384]{0,1:T(8,128)}), f32[4096,384]{0,1:T(8,128)}) %all-gather.9.cloned.1.call-update) | async-done | bytes 6291472 | tf_op jit(solution)/shard_map/all_gather | solution.py:84
  191.9 8.5 %reshape.227 = f32[4,1024,384]{1,0,2:T(4,128)} reshape(f32[4096,384]{0,1:T(8,128)} %all-gather.9.cloned.1.call-done) | data formatting | bytes 12582912 | tf_op jit(solution)/shard_map/all_gather | solution.py:84
  200.5 6.6 %reduce_sum.37 = f32[1024,384]{0,1:T(8,128)S(1)} reduce(f32[4,1024,384]{1,0,2:T(4,128)} %reshape.227, f32[]{:T(128)} %constant.24.clone.1), dimensions={0}, to_apply=%region_1.2 | reduce | flops 1179648 | bytes 7864324 | tf_op jit(solution)/shard_map/reduce_sum | solution.py:85
  207.3 1.2 fusion.32
  208.5 128.6 %reduce-scatter.3.cloned.1.call-done = f32[256,2048]{1,0:T(8,128)} async-done(((f32[1024,2048]{1,0:T(8,128)}), f32[256,2048]{1,0:T(8,128)}) %reduce-scatter.3.cloned.1.call-update) | async-done | bytes 2097168 | tf_op jit(solution)/shard_map/reduce_scatter | solution.py:99
  337.1 1.8 multiply_bitcast_fusion
  338.9 0.4 copy.33
  339.3 0.7 fusion.50
  340.0 1.4 subtract_convert_fusion
  341.3 1.3 fusion.19
  342.7 4.5 fusion.51
  347.2 1.7 fusion.18
  349.0 81.3 %all-gather.7.cloned.1.call-done = bf16[1024,2048]{0,1:T(8,128)(2,1)} async-done(((bf16[256,2048]{0,1:T(8,128)(2,1)}), bf16[1024,2048]{0,1:T(8,128)(2,1)}) %all-gather.7.cloned.1.call-update) | async-done | bytes 4194320 | tf_op jit(solution)/shard_map/all_gather | solution.py:113
  430.3 23.2 %convolution_convert_fusion = bf16[1024,4096]{1,0:T(8,128)(2,1)} fusion(bf16[1024,2048]{0,1:T(8,128)(2,1)} %all-gather.7.cloned.1.call-done, bf16[2048,4096]{1,0:T(8,128)(2,1)} %param.13), kind=kOutput, calls=%fused_computation.8 | convolution fusion | flops 17184063488 | bytes 29360128 | tf_op jit(solution)/shard_map/dot_general | solution.py:116
  453.6 0.7 copy-done.4
  454.2 69.2 %reduce-scatter.5.cloned.1.call-done = bf16[128,4096]{1,0:T(8,128)(2,1)} async-done(((bf16[1024,4096]{1,0:T(8,128)(2,1)}), bf16[128,4096]{1,0:T(8,128)(2,1)}) %reduce-scatter.5.cloned.1.call-update) | async-done | bytes 1048592 | tf_op jit(solution)/shard_map/reduce_scatter | solution.py:115
  523.4 1.7 fusion.12
  525.1 11.7 %psum.7 = f32[128]{0:T(128)S(1)} all-reduce(f32[128]{0:T(128)S(1)} %get-tuple-element.2), channel_id=1, replica_groups=mesh['wa'=4,'ha'=8] {'wa'}, use_global_device_ids=true, to_apply=%region_9.10 | all-reduce | flops 128 | bytes 1024 | tf_op jit(solution)/shard_map/psum | solution.py:123
  536.8 1.3 fusion.14
  (35 shorter events, 1.3 us)
Async XLA Ops:
  7.2 59.7 %all-gather.5.cloned.1.call-start = ((), (), s32[]{:S(2)}) async-start(), calls=%async_computation.2 | async-start | bytes 9437184 | tf_op jit(solution)/shard_map/all_gather | solution.py:78
  7.9 184.0 %all-gather.9.cloned.1.call-start = ((), (), s32[]{:S(2)}) async-start(), calls=%async_computation.6 | async-start | bytes 7864320 | tf_op jit(solution)/shard_map/all_gather | solution.py:84
  66.9 5.8 %copy-start = (bf16[1024,4096]{1,0:T(8,128)(2,1)S(1)}, bf16[1024,4096]{1,0:T(8,128)(2,1)}, u32[]{:S(2)}) copy-start(bf16[1024,4096]{1,0:T(8,128)(2,1)} %all-gather.5.cloned.1.call-done) | copy-start | bytes 25165828
  76.4 260.7 %reduce-scatter.3.cloned.1.call-start = ((), (), s32[]{:S(2)}) async-start(), calls=%async_computation.3 | async-start | bytes 10485760 | tf_op jit(solution)/shard_map/reduce_scatter | solution.py:99
  100.6 0.7 copy-start.3
  100.6 329.7 %all-gather.7.cloned.1.call-start = ((), (), s32[]{:S(2)}) async-start(), calls=%async_computation.4 | async-start | bytes 5242880 | tf_op jit(solution)/shard_map/all_gather | solution.py:113
  349.0 174.4 %reduce-scatter.5.cloned.1.call-start = ((), (), s32[]{:S(2)}) async-start(), calls=%async_computation.5 | async-start | bytes 9437184 | tf_op jit(solution)/shard_map/reduce_scatter | solution.py:115
  453.5 0.7 copy-start.4
  453.5 69.9 %copy-start.2 = (bf16[128,4096]{1,0:T(8,128)(2,1)S(1)}, bf16[128,4096]{1,0:T(8,128)(2,1)}, u32[]{:S(2)}) copy-start(bf16[128,4096]{1,0:T(8,128)(2,1)} %param.8) | copy-start | bytes 3145732
  525.1 13.0 %copy-start.1 = (bf16[128,4096]{1,0:T(8,128)(2,1)}, bf16[128,4096]{1,0:T(8,128)(2,1)S(1)}, u32[]{:S(2)}) copy-start(bf16[128,4096]{1,0:T(8,128)(2,1)S(1)} %get-tuple-element.3) | copy-start | bytes 3145732
Sparse Core Ops, SparseCore 0:
  9.9 56.9 all-gather.4
  76.6 115.3 all-gather.8
  194.3 142.7 reduce-scatter.2
  349.1 81.1 all-gather.6
  453.7 69.6 reduce-scatter.4
